TPU v7x, 512 devices: a whole 4x8x8 slice. The times are simulated.
512 devices in a mesh: tile: 32 (over x, z), row: 16 (over y, core).
Axes of the slice: x: 4, y: 8, z: 8, core: 2. Of those that a mesh axis runs over, the one named last changes fastest.
Arguments:
- voltage: float32 [32, 16, 1, 64, 128], P('tile', 'row'), may hold values from -6 to 6
- history: bfloat16 [32, 16, 32, 64, 128], P('tile', 'row'), may hold values from -6 to 6
- far_blocks: bfloat16 [32, 16, 32, 128, 128], P('tile', 'row'), may hold values from -0.09375 to 0.09375
- far_target: int32 [32, 16, 32, 1], P('tile', 'row'), may hold values from 0 to 31; in each aligned block of 32 rows (0 to 31, 32 to 63, ..., all dimensions but the last counted through in order) at most 2 rows name the same one
- far_delay: int32 [32, 16, 32], P('tile', 'row'), may hold values from 1 to 32
- near_blocks: bfloat16 [32, 16, 3, 128, 128], P('tile', 'row'), may hold values from -0.15625 to 0.15625
- near_link: int32 [32, 16, 2], P('tile', 'row'), may hold values 0 or 1
- jacobi_blocks: bfloat16 [32, 16, 128, 128], P('tile', 'row'), may hold values from -0.21875 to 0.21875
Outputs:
- currents: float32 [32, 16, 1, 64, 128], P('tile', 'row')
Inputs may be any that keep to these rules, and one draw needn't show every extreme that they name: `far_target`: among the 32 entries of one tile at most 2 name the same target, and some tile has exactly 2 naming one target.
All inputs are finite; a program needn't handle non-finite values. No bound on the sum of `near_link` on one device may be relied on, other than what follows from the above.
Results may differ from a plain program's by a relative error of at most 0.0003.
Values sent between devices are 32-bit elements; how exact they have to be, the bound alone decides.
No kernel may reach another device: no remote copies, remote signals or barrier semaphores. Data moves between devices by JAX's collectives and lax.ppermute only.
A program may use at most 64 MiB of HBM per device.

v0:
```python
import jax
import jax.numpy as jnp
from jax import lax
from jax.sharding import PartitionSpec as P

ITERS = 5
PRECISE = lax.Precision.HIGHEST


def padded_2(array, sides, width):
    for axis, dim in sides:
        size, length = (lax.axis_size(axis), array.shape[dim])
        up = [(i, (i + 1) % size) for i in range(size - 1)]
        down = [(j, i) for i, j in up]
        last = lax.slice_in_dim(array, length - width, length, axis=dim)
        first = lax.slice_in_dim(array, 0, width, axis=dim)
        before = lax.ppermute(last, axis, up)
        after = lax.ppermute(first, axis, down)
        array = jnp.concatenate([before, array, after], axis=dim)
    return array


def near_apply(field, near_f32, link_gain):
    padded = padded_2(field[None], (("row", 0),), 1)
    result = field + jnp.dot(field, near_f32[1], precision=PRECISE)
    result = result + link_gain[0] * jnp.dot(padded[0], near_f32[0], precision=PRECISE)
    result = result + link_gain[1] * jnp.dot(padded[2], near_f32[2], precision=PRECISE)
    return result


def jacobi_apply(field, jacobi_f32):
    return field + jnp.dot(field, jacobi_f32, precision=PRECISE)


def givens_solve(hessen, start_norm, iterations):
    matrix = [[hessen[i][k] for k in range(iterations)] for i in range(iterations + 1)]
    target = [start_norm] + [jnp.zeros_like(start_norm) for k in range(iterations)]
    for j in range(iterations):
        diag_val = matrix[j][j]
        below_val = matrix[j + 1][j]
        radius = jnp.sqrt(diag_val * diag_val + below_val * below_val)
        cosine = diag_val / radius
        sine_val = below_val / radius
        for k in range(j, iterations):
            upper_val = matrix[j][k]
            lower_val = matrix[j + 1][k]
            matrix[j][k] = cosine * upper_val + sine_val * lower_val
            matrix[j + 1][k] = cosine * lower_val - sine_val * upper_val
        target[j + 1] = -sine_val * target[j]
        target[j] = cosine * target[j]
    coeffs = [None] * iterations
    for j in reversed(range(iterations)):
        partial_val = target[j]
        for k in range(j + 1, iterations):
            partial_val = partial_val - matrix[j][k] * coeffs[k]
        coeffs[j] = partial_val / matrix[j][j]
    return coeffs


def krylov_solve(right_side, near_f32, link_gain, jacobi_f32):
    initial = jacobi_apply(right_side, jacobi_f32)
    start_sq = lax.psum(jnp.sum(initial * initial, axis=1), ("tile", "row"))
    start_norm = jnp.sqrt(start_sq)
    basis = [initial / start_norm[:, None]]
    zero_row = jnp.zeros_like(start_norm)
    hessen = [[zero_row for k in range(ITERS)] for i in range(ITERS + 1)]
    for j in range(ITERS):
        candidate = jacobi_apply(near_apply(basis[j], near_f32, link_gain), jacobi_f32)
        local_dots = jnp.stack([jnp.sum(v * candidate, axis=1) for v in basis])
        projections = lax.psum(local_dots, ("tile", "row"))
        for i in range(j + 1):
            candidate = candidate - projections[i][:, None] * basis[i]
        new_sq = lax.psum(jnp.sum(candidate * candidate, axis=1), ("tile", "row"))
        new_norm = jnp.sqrt(new_sq)
        for i in range(j + 1):
            hessen[i][j] = projections[i]
        hessen[j + 1][j] = new_norm
        basis.append(candidate / new_norm[:, None])
    coeffs = givens_solve(hessen, start_norm, ITERS)
    result = coeffs[0][:, None] * basis[0]
    for j in range(1, ITERS):
        result = result + coeffs[j][:, None] * basis[j]
    return result


def per_device(
    voltage, history, far_blocks, far_target, far_delay, near_blocks, near_link, jacobi_blocks
):
    voltage = voltage[0, 0]
    history = history[0, 0]
    far_blocks = far_blocks[0, 0]
    targets = far_target[0, 0, :, 0]
    delays = far_delay[0, 0]
    near_f32 = near_blocks[0, 0].astype(jnp.float32)
    link_gain = near_link[0, 0].astype(jnp.float32)
    jacobi_f32 = jacobi_blocks[0, 0].astype(jnp.float32)
    tile_count = lax.axis_size("tile")
    entries = far_blocks.shape[0]
    capacity = max(2, entries // tile_count + 1)
    scenarios = voltage.shape[1]
    segments = voltage.shape[2]
    ordinal = jnp.arange(entries, dtype=jnp.int32)
    earlier = (ordinal[:, None] > ordinal[None, :]) & (targets[:, None] == targets[None, :])
    ranking = jnp.sum(earlier.astype(jnp.int32), axis=1)
    destination = targets * capacity + ranking
    placing = (
        jnp.arange(tile_count * capacity, dtype=jnp.int32)[:, None] == destination[None, :]
    ).astype(jnp.float32)
    currents = []
    pieces = [c.astype(jnp.bfloat16)[None] for c in reversed(currents)]
    stacked = jnp.concatenate(pieces + [history], axis=0)
    chosen = jnp.take(stacked, delays - 1, axis=0)
    products = jnp.einsum("lcs,lst->lct", chosen, far_blocks, preferred_element_type=jnp.float32)
    flattened = products.reshape(entries, scenarios * segments)
    bucket = jnp.dot(placing, flattened, precision=PRECISE).reshape(
        tile_count, capacity, scenarios, segments
    )
    received = lax.all_to_all(bucket, "tile", split_axis=0, concat_axis=0, tiled=True)
    far_field = jnp.sum(received, axis=(0, 1))
    right_side = voltage[0] - far_field
    currents.append(krylov_solve(right_side, near_f32, link_gain, jacobi_f32))
    return jnp.stack(currents)[None, None]


def solution(mesh):
    return jax.shard_map(
        per_device,
        mesh=mesh,
        in_specs=(
            P("tile", "row", None, None, None),
            P("tile", "row", None, None, None),
            P("tile", "row", None, None, None),
            P("tile", "row", None, None),
            P("tile", "row", None),
            P("tile", "row", None, None, None),
            P("tile", "row", None),
            P("tile", "row", None, None),
        ),
        out_specs=P("tile", "row", None, None, None),
        check_vma=False,
    )
```

profile of v0, /device:TPU:1, one launch (start us, length us, event | category | flops | bytes accessed | tf_op | source)
XLA Modules:
  0.0 1178.2 jit_solution(18012329410993611256)
XLA Ops:
  0.0 0.7 fusion.70
  0.8 0.7 compare_and_fusion
  1.4 0.9 convert_reduce_fusion
  2.3 0.7 multiply_add_fusion.1
  3.0 1.7 gather_fusion
  4.7 0.5 fusion.12
  5.2 1.7 fusion.10
  6.9 2.6 copy.13
  9.4 13.8 %all-to-all-start = ((f32[32,2,64,128]{3,2,1,0:T(8,128)}), f32[32,2,64,128]{3,2,1,0:T(8,128)S(1)}, u32[]{:S(2)}, u32[]{:S(2)}) async-start(f32[32,2,64,128]{3,2,1,0:T(8,128)} %copy.13), calls=%async_computation | async-start | bytes 4194304 | tf_op jit(solution)/shard_map/all_to_all | solution.py:118
  23.3 0.6 fusion.89
  23.9 48.2 %all-to-all-done = f32[32,2,64,128]{3,2,1,0:T(8,128)S(1)} async-done(((f32[32,2,64,128]{3,2,1,0:T(8,128)}), f32[32,2,64,128]{3,2,1,0:T(8,128)S(1)}, u32[]{:S(2)}, u32[]{:S(2)}) %all-to-all-start) | async-done | bytes 2097184 | tf_op jit(solution)/shard_map/all_to_all | solution.py:118
  72.3 0.3 multiply_reduce_fusion.20
  72.6 98.6 %psum.77 = f32[64]{0:T(128)S(1)} all-reduce(f32[64]{0:T(128)S(1)} %get-tuple-element.55), channel_id=1, replica_groups=mesh['tile'=32,'row'=16] {'tile','row'}, use_global_device_ids=true, to_apply=%region_3.4 | all-reduce | flops 64 | bytes 512 | tf_op jit(solution)/shard_map/psum | solution.py:62
  171.3 3.0 collective-permute-start
  174.2 1.9 collective-permute-start.1
  176.2 0.2 convolution_add_fusion.9
  176.4 0.8 fusion.9
  177.2 2.3 collective-permute-done.1
  179.5 0.8 fusion.8
  180.3 0.3 multiply_reduce_fusion.19
  180.5 95.9 %psum.78 = f32[64]{0:T(128)S(1)} all-reduce(f32[64]{0:T(128)S(1)} %get-tuple-element.57), channel_id=1, replica_groups=mesh['tile'=32,'row'=16] {'tile','row'}, use_global_device_ids=true, to_apply=%region_5.6 | all-reduce | flops 64 | bytes 512 | tf_op jit(solution)/shard_map/psum | solution.py:70
  276.5 0.2 multiply_reduce_fusion.18
  276.6 95.5 %psum.79 = f32[64]{0:T(128)S(1)} all-reduce(f32[64]{0:T(128)S(1)} %multiply_reduce_fusion.18), channel_id=1, replica_groups=mesh['tile'=32,'row'=16] {'tile','row'}, use_global_device_ids=true, to_apply=%region_7.8 | all-reduce | flops 64 | bytes 512 | tf_op jit(solution)/shard_map/psum | solution.py:73
  372.3 2.7 collective-permute-start.2
  375.0 0.2 convolution_add_fusion.7
  375.2 1.9 collective-permute-start.3
  377.1 0.8 fusion.7
  377.9 2.5 collective-permute-done.3
  380.4 0.8 fusion.6
  381.2 0.3 multiply_reduce_fusion.17
  381.5 95.9 %psum.80 = f32[2,64]{1,0:T(2,128)S(1)} all-reduce(f32[2,64]{1,0:T(2,128)S(1)} %pad_maximum_fusion.2), channel_id=1, replica_groups=mesh['tile'=32,'row'=16] {'tile','row'}, use_global_device_ids=true, to_apply=%region_10.11 | all-reduce | flops 128 | bytes 1024 | tf_op jit(solution)/shard_map/psum | solution.py:70
  477.5 0.2 multiply_reduce_fusion.15
  477.7 95.3 %psum.81 = f32[64]{0:T(128)S(1)} all-reduce(f32[64]{0:T(128)S(1)} %get-tuple-element.34), channel_id=1, replica_groups=mesh['tile'=32,'row'=16] {'tile','row'}, use_global_device_ids=true, to_apply=%region_12.13 | all-reduce | flops 64 | bytes 512 | tf_op jit(solution)/shard_map/psum | solution.py:73
  573.0 3.3 collective-permute-start.4
  576.4 0.2 convolution_add_fusion.5
  576.6 1.9 collective-permute-start.5
  578.6 0.8 fusion.5
  579.3 2.5 collective-permute-done.5
  581.8 0.8 fusion.4
  582.7 0.3 multiply_reduce_fusion.14
  583.0 96.0 %psum.82 = f32[3,64]{1,0:T(4,128)S(1)} all-reduce(f32[3,64]{1,0:T(4,128)S(1)} %pad_maximum_fusion), channel_id=1, replica_groups=mesh['tile'=32,'row'=16] {'tile','row'}, use_global_device_ids=true, to_apply=%region_16.17 | all-reduce | flops 192 | bytes 1536 | tf_op jit(solution)/shard_map/psum | solution.py:70
  679.0 0.2 multiply_reduce_fusion.11
  679.2 95.1 %psum.83 = f32[64]{0:T(128)S(1)} all-reduce(f32[64]{0:T(128)S(1)} %get-tuple-element.32), channel_id=1, replica_groups=mesh['tile'=32,'row'=16] {'tile','row'}, use_global_device_ids=true, to_apply=%region_18.19 | all-reduce | flops 64 | bytes 512 | tf_op jit(solution)/shard_map/psum | solution.py:73
  774.4 0.2 convolution_add_fusion.3
  774.6 3.1 collective-permute-start.6
  777.7 2.1 collective-permute-start.7
  779.9 0.8 fusion.3
  780.7 2.3 collective-permute-done.7
  782.9 0.8 fusion.2
  783.8 0.3 multiply_reduce_fusion.10
  784.1 96.8 %psum.84 = f32[4,64]{1,0:T(4,128)S(1)} all-reduce(f32[4,64]{1,0:T(4,128)S(1)} %pad_maximum_fusion.1), channel_id=1, replica_groups=mesh['tile'=32,'row'=16] {'tile','row'}, use_global_device_ids=true, to_apply=%region_23.24 | all-reduce | flops 256 | bytes 2048 | tf_op jit(solution)/shard_map/psum | solution.py:70
  880.9 0.2 multiply_reduce_fusion.6
  881.1 94.5 %psum.85 = f32[64]{0:T(128)S(1)} all-reduce(f32[64]{0:T(128)S(1)} %get-tuple-element.30), channel_id=1, replica_groups=mesh['tile'=32,'row'=16] {'tile','row'}, use_global_device_ids=true, to_apply=%region_25.26 | all-reduce | flops 64 | bytes 512 | tf_op jit(solution)/shard_map/psum | solution.py:73
  975.7 3.3 collective-permute-start.8
  979.0 0.2 convolution_add_fusion.1
  979.2 1.9 collective-permute-start.9
  981.1 0.8 fusion.1
  981.9 2.5 collective-permute-done.9
  984.4 0.8 fusion
  985.2 0.3 multiply_reduce_fusion.1
  985.6 96.2 %psum.86 = f32[5,64]{1,0:T(8,128)S(1)} all-reduce(f32[5,64]{1,0:T(8,128)S(1)} %stack.75), channel_id=1, replica_groups=mesh['tile'=32,'row'=16] {'tile','row'}, use_global_device_ids=true, to_apply=%region_31.32 | all-reduce | flops 320 | bytes 2560 | tf_op jit(solution)/shard_map/psum | solution.py:70
  1081.9 0.2 multiply_reduce_fusion
  1082.1 95.2 %psum.87 = f32[64]{0:T(128)S(1)} all-reduce(f32[64]{0:T(128)S(1)} %multiply_reduce_fusion), channel_id=1, replica_groups=mesh['tile'=32,'row'=16] {'tile','row'}, use_global_device_ids=true, to_apply=%region_33.34 | all-reduce | flops 64 | bytes 512 | tf_op jit(solution)/shard_map/psum | solution.py:73
  1177.5 0.8 add_bitcast_fusion
  (40 shorter events, 0.9 us)
Async XLA Ops:
  0.0 4.7 copy-start
  9.4 13.9 %copy-start.4 = (s32[1,1,2]{2,1,0:T(1,128)S(1)}, s32[1,1,2]{2,1,0:T(1,128)}, u32[]{:S(2)}) copy-start(s32[1,1,2]{2,1,0:T(1,128)} %param.14) | copy-start | bytes 28
  9.4 62.7 %all-to-all-start = ((f32[32,2,64,128]{3,2,1,0:T(8,128)}), f32[32,2,64,128]{3,2,1,0:T(8,128)S(1)}, u32[]{:S(2)}, u32[]{:S(2)}) async-start(f32[32,2,64,128]{3,2,1,0:T(8,128)} %copy.13), calls=%async_computation | async-start | bytes 4194304 | tf_op jit(solution)/shard_map/all_to_all | solution.py:118
  23.3 49.0 %copy-start.2 = (f32[1,1,1,64,128]{4,3,2,1,0:T(8,128)S(1)}, f32[1,1,1,64,128]{4,3,2,1,0:T(8,128)}, u32[]{:S(2)}) copy-start(f32[1,1,1,64,128]{4,3,2,1,0:T(8,128)} %param.8) | copy-start | bytes 98308
  23.3 49.0 %copy-start.3 = (bf16[1,1,128,128]{3,2,1,0:T(8,128)(2,1)S(1)}, bf16[1,1,128,128]{3,2,1,0:T(8,128)(2,1)}, u32[]{:S(2)}) copy-start(bf16[1,1,128,128]{3,2,1,0:T(8,128)(2,1)} %param.15) | copy-start | bytes 98308
  23.3 152.8 %copy-start.1 = (bf16[1,1,3,128,128]{4,3,2,1,0:T(8,128)(2,1)S(1)}, bf16[1,1,3,128,128]{4,3,2,1,0:T(8,128)(2,1)}, u32[]{:S(2)}) copy-start(bf16[1,1,3,128,128]{4,3,2,1,0:T(8,128)(2,1)} %param.13) | copy-start | bytes 294916
  171.3 5.1 collective-permute-start
  174.2 5.2 collective-permute-start.1
  372.3 4.8 collective-permute-start.2
  375.2 5.2 collective-permute-start.3
  573.0 5.5 collective-permute-start.4
  576.6 5.2 collective-permute-start.5
  774.6 5.2 collective-permute-start.6
  777.7 5.2 collective-permute-start.7
  975.7 5.4 collective-permute-start.8
  979.2 5.2 collective-permute-start.9
where the time goes:
time: 1180 us
  blocking collectives  1060 us (90%)
  waiting for transfers between devices  60.3 us (5%)
  starting transfers between devices  38.9 us (3%)
  matrix products  12.9 us (1%)
    psum x5, blocking collectives, krylov_solve(): projections = lax.psum(local_dots, ('tile', 'row'))  481 us
    psum x5, blocking collectives, krylov_solve(): new_sq = lax.psum(jnp.sum(candidate * candidate, axis=1), ('tile', 'row'))  476 us
    psum x1, blocking collectives, krylov_solve(): start_sq = lax.psum(jnp.sum(initial * initial, axis=1), ('tile', 'row'))  98.6 us
    all_to_all x1, waiting for transfers between devices, per_device(): lax.all_to_all(bucket, 'tile', split_axis=0, concat_axis=0, tiled=True)  48.2 us
  transfers between devices with their start and end apart: 11, of which 6 were waited for; matrix products, arithmetic and copies ran while one was open for 0% of the time, Pallas kernels for 0%

commit v1 on v0

--- a/solution.py
+++ b/solution.py
@@ -67,7 +67,7 @@
     for j in range(ITERS):
         candidate = jacobi_apply(near_apply(basis[j], near_f32, link_gain), jacobi_f32)
         local_dots = jnp.stack([jnp.sum(v * candidate, axis=1) for v in basis])
-        projections = lax.psum(local_dots, ("tile", "row"))
+        projections = jnp.sum(lax.all_gather(local_dots, ("tile", "row")), axis=0)
         for i in range(j + 1):
             candidate = candidate - projections[i][:, None] * basis[i]
         new_sq = lax.psum(jnp.sum(candidate * candidate, axis=1), ("tile", "row"))

time: 1180 us -> 1250 us (1.059)
  waiting for transfers between devices: 60.3 us -> 318 us
  blocking collectives: 1060 us -> 853 us
  between operations: 0.44 us -> 13.9 us
    psum x5 -> x0, blocking collectives: 481 us -> none  [krylov_solve(): projections = lax.psum(local_dots, ('tile', 'row'))]
    all_gather x0 -> x4, blocking collectives: none -> 279 us  [krylov_solve(): projections = jnp.sum(lax.all_gather(local_dots, ('tile', 'row')), axis=0)]
    unnamed x0 -> x2, waiting for transfers between devices: none -> 258 us
  transfers between devices with their start and end apart: 11 -> 12, of which waited for: 6 -> 7; matrix products, arithmetic and copies ran while one was open for 0% -> 0% of each run, Pallas kernels for 0% -> 0%
where the time goes in v1:
time: 1250 us
  blocking collectives  853 us (68%)
  waiting for transfers between devices  318 us (25%)
  starting transfers between devices  40.3 us (3%)
  between operations  13.9 us (1%)
  matrix products  12.9 us (1%)
    psum x5, blocking collectives, krylov_solve(): new_sq = lax.psum(jnp.sum(candidate * candidate, axis=1), ('tile', 'row'))  476 us
    all_gather x4, blocking collectives, krylov_solve(): projections = jnp.sum(lax.all_gather(local_dots, ('tile', 'row')), axis=0)  279 us
    unnamed x2, waiting for transfers between devices  258 us
    psum x1, blocking collectives, krylov_solve(): start_sq = lax.psum(jnp.sum(initial * initial, axis=1), ('tile', 'row'))  98.6 us
    all_to_all x1, waiting for transfers between devices, per_device(): lax.all_to_all(bucket, 'tile', split_axis=0, concat_axis=0, tiled=True)  48.2 us
  transfers between devices with their start and end apart: 12, of which 7 were waited for; matrix products, arithmetic and copies ran while one was open for 0% of the time, Pallas kernels for 0%

profile of v1, /device:TPU:1, one launch (start us, length us, event | category | flops | bytes accessed | tf_op | source)
XLA Modules:
  0.0 1253.0 jit_solution(11528460509925113692)
XLA Ops:
  6.5 0.7 fusion.70
  7.3 0.7 compare_and_fusion
  8.0 0.9 convert_reduce_fusion
  8.9 0.7 multiply_add_fusion.1
  9.5 1.7 gather_fusion
  11.2 0.5 fusion.12
  11.7 1.7 fusion.10
  13.4 2.6 copy.13
  16.0 13.8 %all-to-all-start = ((f32[32,2,64,128]{3,2,1,0:T(8,128)}), f32[32,2,64,128]{3,2,1,0:T(8,128)S(1)}, u32[]{:S(2)}, u32[]{:S(2)}) async-start(f32[32,2,64,128]{3,2,1,0:T(8,128)} %copy.13), calls=%async_computation | async-start | bytes 4194304 | tf_op jit(solution)/shard_map/all_to_all | solution.py:118
  29.9 0.6 fusion.89
  30.5 48.2 %all-to-all-done = f32[32,2,64,128]{3,2,1,0:T(8,128)S(1)} async-done(((f32[32,2,64,128]{3,2,1,0:T(8,128)}), f32[32,2,64,128]{3,2,1,0:T(8,128)S(1)}, u32[]{:S(2)}, u32[]{:S(2)}) %all-to-all-start) | async-done | bytes 2097184 | tf_op jit(solution)/shard_map/all_to_all | solution.py:118
  78.8 0.3 multiply_reduce_fusion.20
  79.1 98.6 %psum.42 = f32[64]{0:T(128)S(1)} all-reduce(f32[64]{0:T(128)S(1)} %get-tuple-element.55), channel_id=1, replica_groups=mesh['tile'=32,'row'=16] {'tile','row'}, use_global_device_ids=true, to_apply=%region_3.4 | all-reduce | flops 64 | bytes 512 | tf_op jit(solution)/shard_map/psum | solution.py:62
  177.8 2.9 collective-permute-start
  180.8 1.9 collective-permute-start.1
  182.7 0.2 convolution_add_fusion.9
  182.9 0.8 fusion.9
  183.7 2.3 collective-permute-done.1
  186.0 0.8 fusion.8
  186.8 0.3 multiply_reduce_fusion.19
  187.1 0.3 dynamic-update-slice
  187.4 0.7 copy-done.2
  188.1 257.9 %all-reduce.3.cloned.1.call-done = f32[32768]{0:T(1024)} async-done(((f32[32768]{0:T(1024)}), f32[32768]{0:T(1024)}) %all-reduce.3.cloned.1.call-update) | async-done | bytes 131088
  446.0 1.0 reshape.122
  447.2 95.1 %psum.43 = f32[64]{0:T(128)S(1)} all-reduce(f32[64]{0:T(128)S(1)} %multiply_reduce_fusion.18), channel_id=1, replica_groups=mesh['tile'=32,'row'=16] {'tile','row'}, use_global_device_ids=true, to_apply=%region_7.8 | all-reduce | flops 64 | bytes 512 | tf_op jit(solution)/shard_map/psum | solution.py:73
  542.4 3.3 collective-permute-start.2
  545.9 1.9 collective-permute-start.3
  547.9 0.8 fusion.7
  548.6 2.5 collective-permute-done.3
  551.2 0.8 fusion.6
  552.0 0.3 multiply_reduce_fusion.17
  552.3 65.7 %all-gather.5 = f32[512,2,64]{2,1,0:T(2,128)S(1)} all-gather(f32[1,2,64]{2,1,0:T(2,128)S(1)} %maximum_bitcast_fusion.2), channel_id=3, replica_groups=mesh['tile'=32,'row'=16] {'tile','row'}, dimensions={0}, use_global_device_ids=true | all-gather | bytes 262656 | tf_op jit(solution)/shard_map/all_gather | solution.py:70
  617.9 0.5 reduce_sum.263
  618.7 95.5 %psum.44 = f32[64]{0:T(128)S(1)} all-reduce(f32[64]{0:T(128)S(1)} %get-tuple-element.34), channel_id=1, replica_groups=mesh['tile'=32,'row'=16] {'tile','row'}, use_global_device_ids=true, to_apply=%region_12.13 | all-reduce | flops 64 | bytes 512 | tf_op jit(solution)/shard_map/psum | solution.py:73
  714.3 3.2 collective-permute-start.4
  717.7 1.9 collective-permute-start.5
  719.7 0.8 fusion.5
  720.5 2.5 collective-permute-done.5
  723.0 0.8 fusion.4
  723.8 0.3 multiply_reduce_fusion.14
  724.1 72.7 %all-gather.6 = f32[512,3,64]{2,1,0:T(4,128)S(1)} all-gather(f32[1,3,64]{2,1,0:T(4,128)S(1)} %maximum_bitcast_fusion), channel_id=4, replica_groups=mesh['tile'=32,'row'=16] {'tile','row'}, dimensions={0}, use_global_device_ids=true | all-gather | bytes 393984 | tf_op jit(solution)/shard_map/all_gather | solution.py:70
  796.8 0.5 reduce_sum.268
  797.5 95.0 %psum.45 = f32[64]{0:T(128)S(1)} all-reduce(f32[64]{0:T(128)S(1)} %get-tuple-element.32), channel_id=1, replica_groups=mesh['tile'=32,'row'=16] {'tile','row'}, use_global_device_ids=true, to_apply=%region_18.19 | all-reduce | flops 64 | bytes 512 | tf_op jit(solution)/shard_map/psum | solution.py:73
  892.7 0.2 convolution_add_fusion.3
  892.9 3.6 collective-permute-start.6
  896.6 1.9 collective-permute-start.7
  898.5 0.8 fusion.3
  899.3 2.5 collective-permute-done.7
  901.8 0.8 fusion.2
  902.6 0.3 multiply_reduce_fusion.10
  902.9 72.5 %all-gather.7 = f32[512,4,64]{2,1,0:T(4,128)S(1)} all-gather(f32[1,4,64]{2,1,0:T(4,128)S(1)} %maximum_bitcast_fusion.1), channel_id=5, replica_groups=mesh['tile'=32,'row'=16] {'tile','row'}, dimensions={0}, use_global_device_ids=true | all-gather | bytes 525312 | tf_op jit(solution)/shard_map/all_gather | solution.py:70
  975.5 0.5 reduce_sum.274
  976.3 95.0 %psum.46 = f32[64]{0:T(128)S(1)} all-reduce(f32[64]{0:T(128)S(1)} %get-tuple-element.30), channel_id=1, replica_groups=mesh['tile'=32,'row'=16] {'tile','row'}, use_global_device_ids=true, to_apply=%region_25.26 | all-reduce | flops 64 | bytes 512 | tf_op jit(solution)/shard_map/psum | solution.py:73
  1071.4 3.7 collective-permute-start.8
  1075.3 1.9 collective-permute-start.9
  1077.2 0.8 fusion.1
  1078.0 2.5 collective-permute-done.9
  1080.5 0.8 fusion
  1081.3 0.4 multiply_reduce_fusion.1
  1081.7 67.8 %all-gather.8 = f32[512,5,64]{2,1,0:T(8,128)S(1)} all-gather(f32[1,5,64]{2,1,0:T(8,128)S(1)} %bitcast.320), channel_id=6, replica_groups=mesh['tile'=32,'row'=16] {'tile','row'}, dimensions={0}, use_global_device_ids=true | all-gather | bytes 656640 | tf_op jit(solution)/shard_map/all_gather | solution.py:70
  1149.5 0.5 reduce_sum.281
  1150.0 0.2 multiply_reduce_fusion
  1150.3 95.0 %psum.47 = f32[64]{0:T(128)S(1)} all-reduce(f32[64]{0:T(128)S(1)} %multiply_reduce_fusion), channel_id=1, replica_groups=mesh['tile'=32,'row'=16] {'tile','row'}, use_global_device_ids=true, to_apply=%region_33.34 | all-reduce | flops 64 | bytes 512 | tf_op jit(solution)/shard_map/psum | solution.py:73
  1245.4 0.8 add_bitcast_fusion
  (52 shorter events, 2.5 us)
Async XLA Ops:
  6.5 4.7 copy-start
  16.0 13.9 %copy-start.5 = (s32[1,1,2]{2,1,0:T(1,128)S(1)}, s32[1,1,2]{2,1,0:T(1,128)}, u32[]{:S(2)}) copy-start(s32[1,1,2]{2,1,0:T(1,128)} %param.14) | copy-start | bytes 28
  16.0 62.7 %all-to-all-start = ((f32[32,2,64,128]{3,2,1,0:T(8,128)}), f32[32,2,64,128]{3,2,1,0:T(8,128)S(1)}, u32[]{:S(2)}, u32[]{:S(2)}) async-start(f32[32,2,64,128]{3,2,1,0:T(8,128)} %copy.13), calls=%async_computation | async-start | bytes 4194304 | tf_op jit(solution)/shard_map/all_to_all | solution.py:118
  29.8 49.0 %copy-start.3 = (f32[1,1,1,64,128]{4,3,2,1,0:T(8,128)S(1)}, f32[1,1,1,64,128]{4,3,2,1,0:T(8,128)}, u32[]{:S(2)}) copy-start(f32[1,1,1,64,128]{4,3,2,1,0:T(8,128)} %param.8) | copy-start | bytes 98308
  29.8 49.0 %copy-start.4 = (bf16[1,1,128,128]{3,2,1,0:T(8,128)(2,1)S(1)}, bf16[1,1,128,128]{3,2,1,0:T(8,128)(2,1)}, u32[]{:S(2)}) copy-start(bf16[1,1,128,128]{3,2,1,0:T(8,128)(2,1)} %param.15) | copy-start | bytes 98308
  29.8 152.8 %copy-start.1 = (bf16[1,1,3,128,128]{4,3,2,1,0:T(8,128)(2,1)S(1)}, bf16[1,1,3,128,128]{4,3,2,1,0:T(8,128)(2,1)}, u32[]{:S(2)}) copy-start(bf16[1,1,3,128,128]{4,3,2,1,0:T(8,128)(2,1)} %param.13) | copy-start | bytes 294916
  29.9 416.1 %all-reduce.3.cloned.1.call-start = ((), (), s32[]{:S(2)}) async-start(), calls=%async_computation.1 | async-start | bytes 262144
  177.8 5.1 collective-permute-start
  180.8 5.2 collective-permute-start.1
  187.4 0.7 copy-start.2
  542.4 5.4 collective-permute-start.2
  545.9 5.2 collective-permute-start.3
  714.3 5.4 collective-permute-start.4
  717.7 5.2 collective-permute-start.5
  892.9 5.6 collective-permute-start.6
  896.6 5.2 collective-permute-start.7
  1071.4 5.9 collective-permute-start.8
  1075.3 5.2 collective-permute-start.9
Sparse Core Ops, SparseCore 0:
  188.2 257.7 all-reduce.2
